TPU v7x, 128 devices: a whole 4x4x4 slice. The times are simulated.
128 devices in a mesh: bucket: 8 (over y, core), member: 16 (over z, x).
Axes of the slice: x: 4, y: 4, z: 4, core: 2. Of those that a mesh axis runs over, the one named last changes fastest.
Arguments:
- loader_rows: float32 [8192, 4096], P(('bucket', 'member')), may hold values from -12 to 12
- dest_bucket: int32 [8192], P(('bucket', 'member')), may hold values from 0 to 7, as said below
- dest_slot: int32 [8192], P(('bucket', 'member')), may hold values from 0 to 127, as said below
- noise: float32 [32768, 4096], P(('bucket', 'member')), may hold values from -12 to 12
Outputs:
- targets: float32 [32768, 4096], P(('bucket', 'member'))
Inputs may be any that keep to these rules, and one draw needn't show every extreme that they name: Loaded row r goes to bucket group dest_bucket[r] on the device of that group with the same member index as its loader device. No loader device sends more than 16 rows to one bucket group; on every member index one bucket group receives exactly 16 rows from every loader device, and every bucket group is so filled on some member index. `dest_slot`: rows that reach the same device have distinct slots.
All inputs are finite; a program needn't handle non-finite values.
Results may differ from a plain program's by a relative error of at most 0.012.
The roundings to bfloat16 on the way count: a program that leaves them out, or rounds other values in their place, can miss the bound.
Values may be sent and summed in bfloat16 or wider, within the bound.
A program may use at most 128 MiB of HBM per device.

v0:
```python
import math
import jax
import jax.numpy as jnp
from jax import lax
from jax.sharding import PartitionSpec as P

ROWS_DEV = 128
ITERS = 4


def tile_cost(panel, noise_rows, noise_norm, width):
    cross_term = lax.dot_general(
        panel, noise_rows, (((1,), (1,)), ((), ())), preferred_element_type=jnp.float32
    )
    panel_wide = panel.astype(jnp.float32)
    return (
        jnp.sum(panel_wide * panel_wide, axis=1)[:, None] + noise_norm[None, :] - 2.0 * cross_term
    ) / width


def body(loader_rows, dest_bucket, dest_slot, noise):
    groups = lax.axis_size("bucket")
    width = loader_rows.shape[1]
    noise_count = noise.shape[0]
    capacity = ROWS_DEV // groups
    epsilon = 0.64 / math.sqrt(width)
    rounded = loader_rows.astype(jnp.bfloat16)
    hits = (dest_bucket[:, None] == jnp.arange(groups, dtype=jnp.int32)[None, :]).astype(jnp.int32)
    ranks = jnp.sum((jnp.cumsum(hits, axis=0) - 1) * hits, axis=1)
    position = dest_bucket * capacity + ranks
    send_rows = jnp.zeros((groups * capacity, width), jnp.bfloat16).at[position].set(rounded)
    send_slots = jnp.full((groups * capacity,), ROWS_DEV, jnp.int32).at[position].set(dest_slot)
    got_rows, got_slots = (
        lax.all_to_all(send_rows, "bucket", split_axis=0, concat_axis=0, tiled=True),
        lax.all_to_all(send_slots, "bucket", split_axis=0, concat_axis=0, tiled=True),
    )
    data_rows = jnp.zeros((ROWS_DEV, width), jnp.bfloat16).at[got_slots].set(got_rows, mode="drop")
    live_rows = (
        jnp.zeros((ROWS_DEV,), jnp.bfloat16)
        .at[got_slots]
        .set(jnp.ones(got_slots.shape, jnp.bfloat16), mode="drop")
    )
    noise_rows = noise.astype(jnp.bfloat16)
    noise_wide = noise_rows.astype(jnp.float32)
    noise_norm = jnp.sum(noise_wide * noise_wide, axis=1)
    whole_rows, whole_live = (
        lax.all_gather(data_rows, "member", axis=0, tiled=True),
        lax.all_gather(live_rows, "member", axis=0, tiled=True),
    )
    cost_tile = tile_cost(whole_rows, noise_rows, noise_norm, width)
    alive_rows = whole_live > 0.5
    col_pot = jnp.zeros((noise_count,), jnp.float32)
    exponent = jnp.zeros(cost_tile.shape, jnp.float32)
    col_total = jnp.ones((noise_count,), jnp.float32)
    for sweep_index in range(ITERS):
        scores = (col_pot[None, :] - cost_tile) / epsilon
        local_peak = jnp.max(scores, axis=1)
        row_peak = lax.pmax(local_peak, "member")
        row_total = lax.psum(jnp.sum(jnp.exp(scores - row_peak[:, None]), axis=1), "member")
        row_pot = -epsilon * (row_peak + jnp.log(row_total))
        col_scores = (row_pot[:, None] - cost_tile) / epsilon
        col_peak = jnp.max(jnp.where(alive_rows[:, None], col_scores, -jnp.inf), axis=0)
        exponent = jnp.where(alive_rows[:, None], jnp.exp(col_scores - col_peak[None, :]), 0.0)
        col_total = jnp.sum(exponent, axis=0)
        col_pot = -epsilon * (col_peak + jnp.log(col_total))
    weights = (exponent / col_total[None, :]).astype(jnp.bfloat16)
    targets = lax.dot_general(
        weights, whole_rows, (((0,), (0,)), ((), ())), preferred_element_type=jnp.float32
    )
    return targets


def solution(mesh):
    return jax.shard_map(
        body,
        mesh=mesh,
        in_specs=(
            P(("bucket", "member"), None),
            P(("bucket", "member")),
            P(("bucket", "member")),
            P(("bucket", "member"), None),
        ),
        out_specs=P(("bucket", "member"), None),
        check_vma=False,
    )
```

profile of v0, /device:TPU:2, one launch (start us, length us, event | category | flops | bytes accessed | tf_op | source)
XLA Modules:
  0.0 500.6 jit_solution(14216818540153028822)
XLA Ops:
  6.5 0.7 fusion.20
  7.4 0.8 select_reduce_fusion.7
  8.9 0.9 scatter_custom_fusion
  10.5 4.5 all-to-all-start
  14.9 3.1 scatter_custom_fusion.2
  18.0 2.2 all-to-all-done
  20.2 3.6 all-to-all-start.1
  25.2 14.4 %all-to-all-done.1 = bf16[8,16,4096]{2,1,0:T(8,128)(2,1)S(1)} async-done(((bf16[8,16,4096]{2,1,0:T(8,128)(2,1)}), bf16[8,16,4096]{2,1,0:T(8,128)(2,1)S(1)}, u32[]{:S(2)}, u32[]{:S(2)}) %all-to-all-start.1) | async-done | bytes 1048608 | tf_op jit(solution)/shard_map/all_to_all | solution.py:34
  39.6 3.0 scatter_custom_fusion.3
  42.7 2.6 multiply_reduce_fusion.1
  45.3 1.3 scatter_custom_fusion.1
  46.6 21.6 %all-gather = bf16[16,1,128]{2,1,0:T(2,128)(2,1)S(1)} all-gather(bf16[1,1,128]{2,1,0:T(2,128)(2,1)S(1)} %bitcast.16), channel_id=1, replica_groups=mesh['bucket'=8,'member'=16] {'member'}, dimensions={0}, use_global_device_ids=true | all-gather | bytes 4352 | tf_op jit(solution)/shard_map/all_gather | solution.py:48
  68.2 86.4 %all-gather.3.cloned.1.call-done = bf16[2048,4096]{1,0:T(8,128)(2,1)} async-done(((bf16[128,4096]{1,0:T(8,128)(2,1)}), bf16[2048,4096]{1,0:T(8,128)(2,1)}) %all-gather.3.cloned.1.call-update) | async-done | bytes 16777232 | tf_op jit(solution)/shard_map/all_gather | solution.py:47
  154.6 7.5 %multiply_reduce_fusion = f32[2048]{0:T(1024)S(1)} fusion(bf16[2048,4096]{1,0:T(8,128)(2,1)} %all-gather.3.cloned.1.call-done), kind=kLoop, calls=%fused_computation.4 | loop fusion | flops 25163776 | bytes 16785408 | tf_op jit(solution)/shard_map/reduce_sum | solution.py:17
  162.1 3.1 copy-done
  165.3 7.8 %fusion.2 = (f32[2048]{0:T(1024)S(1)}, f32[2048,256]{1,0:T(8,128)S(1)}) fusion(bf16[2048,4096]{1,0:T(8,128)(2,1)S(1)} %copy-done, f32[256,4096]{1,0:T(8,128)} %param.7, f32[256]{0:T(256)S(1)} %multiply_reduce_fusion.1, f32[2048]{0:T(1024)S(1)} %multiply_reduce_fusion), kind=kOutput, calls=%fused_computation.30 | convolution fusion | flops 4299683840 | bytes 23086080 | tf_op jit(solution)/shard_map/dot_general | solution.py:12
  173.1 36.8 %pmax.28 = f32[2048]{0:T(1024)S(1)} all-reduce(f32[2048]{0:T(1024)S(1)} %get-tuple-element.5), channel_id=1, replica_groups=mesh['bucket'=8,'member'=16] {'member'}, use_global_device_ids=true, to_apply=%region_9.10 | all-reduce | flops 2048 | bytes 16384 | tf_op jit(solution)/shard_map/pmax | solution.py:58
  209.9 0.8 exponential_reduce_fusion.3
  210.7 38.9 %psum.28 = f32[2048]{0:T(1024)S(1)} all-reduce(f32[2048]{0:T(1024)S(1)} %exponential_reduce_fusion.3), channel_id=1, replica_groups=mesh['bucket'=8,'member'=16] {'member'}, use_global_device_ids=true, to_apply=%region_11.12 | all-reduce | flops 2048 | bytes 16384 | tf_op jit(solution)/shard_map/psum | solution.py:59
  250.3 0.7 select_reduce_fusion.5
  251.4 36.0 %pmax.29 = f32[2048]{0:T(1024)S(1)} all-reduce(f32[2048]{0:T(1024)S(1)} %fusion.3), channel_id=1, replica_groups=mesh['bucket'=8,'member'=16] {'member'}, use_global_device_ids=true, to_apply=%region_15.16 | all-reduce | flops 2048 | bytes 16384 | tf_op jit(solution)/shard_map/pmax | solution.py:58
  287.4 0.8 exponential_reduce_fusion.2
  288.2 38.0 %psum.29 = f32[2048]{0:T(1024)S(1)} all-reduce(f32[2048]{0:T(1024)S(1)} %exponential_reduce_fusion.2), channel_id=1, replica_groups=mesh['bucket'=8,'member'=16] {'member'}, use_global_device_ids=true, to_apply=%region_17.18 | all-reduce | flops 2048 | bytes 16384 | tf_op jit(solution)/shard_map/psum | solution.py:59
  326.9 0.7 select_reduce_fusion.3
  328.0 36.0 %pmax.30 = f32[2048]{0:T(1024)S(1)} all-reduce(f32[2048]{0:T(1024)S(1)} %fusion.4), channel_id=1, replica_groups=mesh['bucket'=8,'member'=16] {'member'}, use_global_device_ids=true, to_apply=%region_21.22 | all-reduce | flops 2048 | bytes 16384 | tf_op jit(solution)/shard_map/pmax | solution.py:58
  364.0 0.8 exponential_reduce_fusion.1
  364.8 38.0 %psum.30 = f32[2048]{0:T(1024)S(1)} all-reduce(f32[2048]{0:T(1024)S(1)} %exponential_reduce_fusion.1), channel_id=1, replica_groups=mesh['bucket'=8,'member'=16] {'member'}, use_global_device_ids=true, to_apply=%region_23.24 | all-reduce | flops 2048 | bytes 16384 | tf_op jit(solution)/shard_map/psum | solution.py:59
  404.7 36.0 %pmax.31 = f32[2048]{0:T(1024)S(1)} all-reduce(f32[2048]{0:T(1024)S(1)} %fusion.5), channel_id=1, replica_groups=mesh['bucket'=8,'member'=16] {'member'}, use_global_device_ids=true, to_apply=%region_27.28 | all-reduce | flops 2048 | bytes 16384 | tf_op jit(solution)/shard_map/pmax | solution.py:58
  440.7 0.8 exponential_reduce_fusion
  441.5 38.2 %psum.31 = f32[2048]{0:T(1024)S(1)} all-reduce(f32[2048]{0:T(1024)S(1)} %exponential_reduce_fusion), channel_id=1, replica_groups=mesh['bucket'=8,'member'=16] {'member'}, use_global_device_ids=true, to_apply=%region_29.30 | all-reduce | flops 2048 | bytes 16384 | tf_op jit(solution)/shard_map/psum | solution.py:59
  480.5 0.7 fusion.6
  481.2 12.6 %fusion.7 = f32[256,4096]{1,0:T(8,128)} fusion(bf16[2048,4096]{1,0:T(8,128)(2,1)} %all-gather.3.cloned.1.call-done, f32[2048,256]{1,0:T(8,128)S(1)} %get-tuple-element.6, f32[256]{0:T(256)S(1)} %fusion.6, f32[256]{0:T(256)S(1)} %select_reduce_fusion, f32[2048]{0:T(1024)S(1)} %add_multiply_fusion, pred[2048]{0:T(1024)(128)(4,1)S(1)} %compare_bitcast_fusion), kind=kOutput, calls=%fused_computation.35 | convolution fusion | flops 4298113024 | bytes 23080960 | tf_op jit(solution)/shard_map/dot_general | solution.py:67
  (27 shorter events, 7.6 us)
Async XLA Ops:
  10.5 9.7 %all-to-all-start = ((s32[8,16,1]{1,2,0:T(1,128)}), s32[8,16,1]{1,2,0:T(1,128)S(1)}, u32[]{:S(2)}, u32[]{:S(2)}) async-start(s32[8,16,1]{1,2,0:T(1,128)} %bitcast), calls=%async_computation | async-start | bytes 8192 | tf_op jit(solution)/shard_map/all_to_all | solution.py:35
  20.2 19.5 %all-to-all-start.1 = ((bf16[8,16,4096]{2,1,0:T(8,128)(2,1)}), bf16[8,16,4096]{2,1,0:T(8,128)(2,1)S(1)}, u32[]{:S(2)}, u32[]{:S(2)}) async-start(bf16[8,16,4096]{2,1,0:T(8,128)(2,1)} %bitcast.4), calls=%async_computation.1 | async-start | bytes 2097152 | tf_op jit(solution)/shard_map/all_to_all | solution.py:34
  23.8 130.8 %all-gather.3.cloned.1.call-start = ((), (), s32[]{:S(2)}) async-start(), calls=%async_computation.2 | async-start | bytes 17825792 | tf_op jit(solution)/shard_map/all_gather | solution.py:47
  154.6 10.7 %copy-start = (bf16[2048,4096]{1,0:T(8,128)(2,1)S(1)}, bf16[2048,4096]{1,0:T(8,128)(2,1)}, u32[]{:S(2)}) copy-start(bf16[2048,4096]{1,0:T(8,128)(2,1)} %all-gather.3.cloned.1.call-done) | copy-start | bytes 50331652
Sparse Core Ops, SparseCore 0:
  42.8 111.7 all-gather.2
where the time goes:
time: 501 us
  blocking collectives  319 us (64%)
  waiting for transfers between devices  103 us (21%)
  other arithmetic  26.2 us (5%)
  matrix products  20.4 us (4%)
  between operations  13.7 us (3%)
  local copies, waits for them, and re-layouts  9.75 us (2%)
  starting transfers between devices  8.07 us (2%)
    psum x4, blocking collectives, body(): lax.psum(jnp.sum(jnp.exp(scores - row_peak[:, None]), axis=1), 'member')  153 us
    pmax x4, blocking collectives, body(): row_peak = lax.pmax(local_peak, 'member')  145 us
    all_gather x1, waiting for transfers between devices, body(): lax.all_gather(data_rows, 'member', axis=0, tiled=True)  86.4 us
    all_gather x1, blocking collectives, body(): lax.all_gather(live_rows, 'member', axis=0, tiled=True)  21.6 us
    all_to_all x1, waiting for transfers between devices, body(): lax.all_to_all(send_rows, 'bucket', split_axis=0, concat_axis=0, tiled=True)  14.4 us
    dot_general x1, matrix products, body(): lax.dot_general(weights, whole_rows, (((0,), (0,)), ((), ())), preferred_...  12.6 us
  transfers between devices with their start and end apart: 3, of which 3 were waited for; matrix products, arithmetic and copies ran while one was open for 2% of the time, Pallas kernels for 0%

commit v1 on v0

--- a/solution.py
+++ b/solution.py
@@ -43,8 +43,21 @@
     noise_rows = noise.astype(jnp.bfloat16)
     noise_wide = noise_rows.astype(jnp.float32)
     noise_norm = jnp.sum(noise_wide * noise_wide, axis=1)
+
+    def get_boxes(vector, dev_axis):
+        h_now = jnp.concatenate(
+            jax.lax.all_to_all(
+                jnp.stack(jax.lax.axis_size(dev_axis) * [vector]),
+                concat_axis=0,
+                split_axis=0,
+                axis_name=dev_axis,
+            ),
+            0,
+        )
+        return h_now
+
     whole_rows, whole_live = (
-        lax.all_gather(data_rows, "member", axis=0, tiled=True),
+        get_boxes(data_rows, "member"),
         lax.all_gather(live_rows, "member", axis=0, tiled=True),
     )
     cost_tile = tile_cost(whole_rows, noise_rows, noise_norm, width)

time: 501 us -> 645 us (1.29)
  blocking collectives: 319 us -> 551 us
  waiting for transfers between devices: 103 us -> 16.7 us
  between operations: 13.7 us -> 0.29 us
  starting transfers between devices: 8.07 us -> 16.4 us
    all_gather x1, blocking collectives: 21.6 us -> 255 us  [body(): lax.all_gather(live_rows, 'member', axis=0, tiled=True)]
    all_gather x1 -> x0, waiting for transfers between devices: 86.4 us -> none  [body(): lax.all_gather(data_rows, 'member', axis=0, tiled=True)]
    all_to_all x0 -> x1, starting transfers between devices: none -> 8.32 us  [get_boxes(): jax.lax.all_to_all(jnp.stack(jax.lax.axis_size(dev_axis) * [vector]), con...]
  transfers between devices with their start and end apart: 3 -> 3, of which waited for: 3 -> 2; matrix products, arithmetic and copies ran while one was open for 2% -> 1% of each run, Pallas kernels for 0% -> 0%
where the time goes in v1:
time: 645 us; the launch traced here: 644 us
  blocking collectives  551 us (85%)
  other arithmetic  26.2 us (4%)
  matrix products  21.1 us (3%)
  waiting for transfers between devices  16.7 us (3%)
  starting transfers between devices  16.4 us (3%)
  local copies, waits for them, and re-layouts  11.9 us (2%)
    all_gather x1, blocking collectives, body(): lax.all_gather(live_rows, 'member', axis=0, tiled=True)  255 us
    psum x4, blocking collectives, body(): lax.psum(jnp.sum(jnp.exp(scores - row_peak[:, None]), axis=1), 'member')  152 us
    pmax x4, blocking collectives, body(): row_peak = lax.pmax(local_peak, 'member')  144 us
    all_to_all x1, waiting for transfers between devices, body(): lax.all_to_all(send_rows, 'bucket', split_axis=0, concat_axis=0, tiled=True)  14.5 us
  transfers between devices with their start and end apart: 3, of which 2 were waited for; matrix products, arithmetic and copies ran while one was open for 1% of the time, Pallas kernels for 0%

profile of v1, /device:TPU:2, one launch (start us, length us, event | category | flops | bytes accessed | tf_op | source)
XLA Modules:
  0.0 643.9 jit_solution(4600688152877593596)
XLA Ops:
  0.0 0.7 fusion.20
  0.8 0.8 select_reduce_fusion.7
  2.3 0.9 scatter_custom_fusion
  3.9 4.5 all-to-all-start
  8.4 3.1 scatter_custom_fusion.2
  11.5 2.2 all-to-all-done
  13.7 3.6 all-to-all-start.1
  18.6 14.5 %all-to-all-done.1 = bf16[8,16,4096]{2,1,0:T(8,128)(2,1)S(1)} async-done(((bf16[8,16,4096]{2,1,0:T(8,128)(2,1)}), bf16[8,16,4096]{2,1,0:T(8,128)(2,1)S(1)}, u32[]{:S(2)}, u32[]{:S(2)}) %all-to-all-start.1) | async-done | bytes 1048608 | tf_op jit(solution)/shard_map/all_to_all | solution.py:34
  33.1 2.3 scatter_custom_fusion.3
  35.4 6.0 stack.2
  41.4 8.3 %all-to-all-start.2 = ((bf16[16,128,4096]{2,1,0:T(8,128)(2,1)}), bf16[16,128,4096]{2,1,0:T(8,128)(2,1)}, u32[]{:S(2)}, u32[]{:S(2)}) async-start(bf16[16,128,4096]{2,1,0:T(8,128)(2,1)} %stack.2), calls=%async_computation.2 | async-start | bytes 33554432 | tf_op jit(solution)/shard_map/all_to_all | solution.py:49
  49.7 2.5 multiply_reduce_fusion.1
  52.3 1.3 scatter_custom_fusion.1
  53.6 255.4 %all-gather = bf16[16,1,128]{2,1,0:T(2,128)(2,1)S(1)} all-gather(bf16[1,1,128]{2,1,0:T(2,128)(2,1)S(1)} %bitcast.15), channel_id=1, replica_groups=mesh['bucket'=8,'member'=16] {'member'}, dimensions={0}, use_global_device_ids=true | all-gather | bytes 4352 | tf_op jit(solution)/shard_map/all_gather | solution.py:61
  309.1 7.5 %multiply_reduce_fusion = f32[16,128]{1,0:T(8,128)S(1)} fusion(bf16[16,128,4096]{2,1,0:T(8,128)(2,1)} %all-to-all-done.2), kind=kLoop, calls=%fused_computation.4 | loop fusion | flops 25163776 | bytes 16785408 | tf_op jit(solution)/shard_map/reduce_sum | solution.py:17
  316.6 8.5 %fusion.2 = (f32[2048]{0:T(1024)S(1)}, f32[2048,256]{1,0:T(8,128)S(1)}) fusion(bf16[2048,4096]{1,0:T(8,128)(2,1)} %bitcast.7, f32[256,4096]{1,0:T(8,128)S(1)} %copy-done, f32[256]{0:T(256)S(1)} %multiply_reduce_fusion.1, f32[2048]{0:T(1024)S(1)} %bitcast.14), kind=kOutput, calls=%fused_computation.30 | convolution fusion | flops 4299683840 | bytes 23086080 | tf_op jit(solution)/shard_map/dot_general | solution.py:12
  325.1 35.6 %pmax.28 = f32[2048]{0:T(1024)S(1)} all-reduce(f32[2048]{0:T(1024)S(1)} %get-tuple-element.5), channel_id=1, replica_groups=mesh['bucket'=8,'member'=16] {'member'}, use_global_device_ids=true, to_apply=%region_9.10 | all-reduce | flops 2048 | bytes 16384 | tf_op jit(solution)/shard_map/pmax | solution.py:71
  360.6 0.8 exponential_reduce_fusion.3
  361.4 38.4 %psum.28 = f32[2048]{0:T(1024)S(1)} all-reduce(f32[2048]{0:T(1024)S(1)} %exponential_reduce_fusion.3), channel_id=1, replica_groups=mesh['bucket'=8,'member'=16] {'member'}, use_global_device_ids=true, to_apply=%region_11.12 | all-reduce | flops 2048 | bytes 16384 | tf_op jit(solution)/shard_map/psum | solution.py:72
  400.5 0.7 select_reduce_fusion.5
  401.6 36.0 %pmax.29 = f32[2048]{0:T(1024)S(1)} all-reduce(f32[2048]{0:T(1024)S(1)} %fusion.3), channel_id=1, replica_groups=mesh['bucket'=8,'member'=16] {'member'}, use_global_device_ids=true, to_apply=%region_15.16 | all-reduce | flops 2048 | bytes 16384 | tf_op jit(solution)/shard_map/pmax | solution.py:71
  437.7 0.8 exponential_reduce_fusion.2
  438.5 38.1 %psum.29 = f32[2048]{0:T(1024)S(1)} all-reduce(f32[2048]{0:T(1024)S(1)} %exponential_reduce_fusion.2), channel_id=1, replica_groups=mesh['bucket'=8,'member'=16] {'member'}, use_global_device_ids=true, to_apply=%region_17.18 | all-reduce | flops 2048 | bytes 16384 | tf_op jit(solution)/shard_map/psum | solution.py:72
  477.4 0.7 select_reduce_fusion.3
  478.5 36.0 %pmax.30 = f32[2048]{0:T(1024)S(1)} all-reduce(f32[2048]{0:T(1024)S(1)} %fusion.4), channel_id=1, replica_groups=mesh['bucket'=8,'member'=16] {'member'}, use_global_device_ids=true, to_apply=%region_21.22 | all-reduce | flops 2048 | bytes 16384 | tf_op jit(solution)/shard_map/pmax | solution.py:71
  514.5 0.8 exponential_reduce_fusion.1
  515.3 38.0 %psum.30 = f32[2048]{0:T(1024)S(1)} all-reduce(f32[2048]{0:T(1024)S(1)} %exponential_reduce_fusion.1), channel_id=1, replica_groups=mesh['bucket'=8,'member'=16] {'member'}, use_global_device_ids=true, to_apply=%region_23.24 | all-reduce | flops 2048 | bytes 16384 | tf_op jit(solution)/shard_map/psum | solution.py:72
  555.1 36.0 %pmax.31 = f32[2048]{0:T(1024)S(1)} all-reduce(f32[2048]{0:T(1024)S(1)} %fusion.5), channel_id=1, replica_groups=mesh['bucket'=8,'member'=16] {'member'}, use_global_device_ids=true, to_apply=%region_27.28 | all-reduce | flops 2048 | bytes 16384 | tf_op jit(solution)/shard_map/pmax | solution.py:71
  591.1 0.8 exponential_reduce_fusion
  591.9 38.0 %psum.31 = f32[2048]{0:T(1024)S(1)} all-reduce(f32[2048]{0:T(1024)S(1)} %exponential_reduce_fusion), channel_id=1, replica_groups=mesh['bucket'=8,'member'=16] {'member'}, use_global_device_ids=true, to_apply=%region_29.30 | all-reduce | flops 2048 | bytes 16384 | tf_op jit(solution)/shard_map/psum | solution.py:72
  630.6 0.7 fusion.6
  631.3 12.6 %fusion.7 = f32[256,4096]{1,0:T(8,128)} fusion(bf16[2048,4096]{1,0:T(8,128)(2,1)} %bitcast.7, f32[2048,256]{1,0:T(8,128)S(1)} %get-tuple-element.6, f32[256]{0:T(256)S(1)} %fusion.6, f32[256]{0:T(256)S(1)} %select_reduce_fusion, f32[2048]{0:T(1024)S(1)} %add_multiply_fusion, pred[2048]{0:T(1024)(128)(4,1)S(1)} %compare_bitcast_fusion), kind=kOutput, calls=%fused_computation.35 | convolution fusion | flops 4298113024 | bytes 23080960 | tf_op jit(solution)/shard_map/dot_general | solution.py:80
  (27 shorter events, 7.5 us)
Async XLA Ops:
  3.9 9.7 %all-to-all-start = ((s32[8,16,1]{1,2,0:T(1,128)}), s32[8,16,1]{1,2,0:T(1,128)S(1)}, u32[]{:S(2)}, u32[]{:S(2)}) async-start(s32[8,16,1]{1,2,0:T(1,128)} %bitcast), calls=%async_computation | async-start | bytes 8192 | tf_op jit(solution)/shard_map/all_to_all | solution.py:35
  13.7 19.5 %all-to-all-start.1 = ((bf16[8,16,4096]{2,1,0:T(8,128)(2,1)}), bf16[8,16,4096]{2,1,0:T(8,128)(2,1)S(1)}, u32[]{:S(2)}, u32[]{:S(2)}) async-start(bf16[8,16,4096]{2,1,0:T(8,128)(2,1)} %bitcast.4), calls=%async_computation.1 | async-start | bytes 2097152 | tf_op jit(solution)/shard_map/all_to_all | solution.py:34
  41.4 267.7 %all-to-all-start.2 = ((bf16[16,128,4096]{2,1,0:T(8,128)(2,1)}), bf16[16,128,4096]{2,1,0:T(8,128)(2,1)}, u32[]{:S(2)}, u32[]{:S(2)}) async-start(bf16[16,128,4096]{2,1,0:T(8,128)(2,1)} %stack.2), calls=%async_computation.2 | async-start | bytes 33554432 | tf_op jit(solution)/shard_map/all_to_all | solution.py:49
  309.1 7.5 %copy-start = (f32[256,4096]{1,0:T(8,128)S(1)}, f32[256,4096]{1,0:T(8,128)}, u32[]{:S(2)}) copy-start(f32[256,4096]{1,0:T(8,128)} %param.7) | copy-start | bytes 12582916
